TPU v7x, 1024 devices: a whole 8x8x8 slice. The times are simulated.
1024 devices in a mesh: grp: 16 (over z, core), dev: 64 (over x, y).
Axes of the slice: x: 8, y: 8, z: 8, core: 2. Of those that a mesh axis runs over, the one named last changes fastest.
Arguments:
- orbitals: bfloat16 [16, 64, 64, 2, 2304], P('grp', 'dev'), may hold values from -6 to 6
- potential: bfloat16 [64, 2304], P('dev'), may hold values from -4 to 4
- counts: int32 [16, 64], P('grp'), may hold values from 16 to 64, as said below
- parity: int32 [16, 64], P('grp', 'dev'), may hold values 0 or 1
Outputs:
- density: float32 [64, 1, 2304], P('dev', None, 'grp')
- filtered: bfloat16 [16, 64, 64, 2, 2304], P('grp', 'dev')
Inputs may be any that keep to these rules, and one draw needn't show every extreme that they name: In each row of 64 fragments the counts sum to 1792, and some fragment of every row holds 64 orbitals and some holds 16.
All inputs are finite; a program needn't handle non-finite values. No bound on the sum of `parity` on one device may be relied on, other than what follows from the above.
Results may differ from a plain program's by a relative error of at most 0.0026.
Values may be sent and summed in bfloat16 or wider, within the bound.
A program may use at most 32 MiB of HBM per device.

v0:
```python
import functools
import math

import jax
import jax.numpy as jnp
from jax import lax
from jax.experimental import pallas as pl
from jax.experimental.pallas import tpu as pltpu
from jax.sharding import PartitionSpec as P

MAXORB = 64
CELLS = 2304
BZ = 48
ROWS = 48
BANDS = 6
TILES = 18
LANES = 128
SHARE = 144
GRP = 16
DEV = 64
ROOTS = [math.cos((2 * i - 1) * math.pi / 16) for i in (1, 8, 4, 5, 2, 7, 3, 6)]
LEAD = 2.0**7 / 7.0**8
MESH = pl.DeviceIdType.MESH
F32 = jnp.float32
BF16 = jnp.bfloat16


def iota(shape, dim):
    return lax.broadcasted_iota(jnp.int32, shape, dim)


def slot_matrix():
    row, lane = iota((LANES, LANES), 0), iota((LANES, LANES), 1)
    return jnp.where((row >> 1) + (row & 1) * MAXORB == lane, 1.0, 0.0).astype(BF16)


def band(ref, y, zi):
    return ref[pl.ds(y * BZ + zi, 8, stride=BANDS), :]


def factor(field, weight, root, with_sum):
    sub = iota((8, LANES), 0)
    first, last = sub == 0, sub == 7
    shift = 7.0 * root
    zero = jnp.zeros((8, LANES), F32)
    before, here = [zero] * BANDS, [band(field, 0, z) for z in range(BANDS)]
    total = zero
    for y in range(ROWS):
        after = [band(field, y + 1, z) for z in range(BANDS)] if y + 1 < ROWS else [zero] * BANDS
        low = jnp.where(first, 0.0, pltpu.roll(here[-1], 1, 0))
        high = jnp.where(last, 0.0, pltpu.roll(here[0], 7, 0))
        wide = [low] + here + [high]
        for z in range(BANDS):
            beside = (wide[z] + wide[z + 2]) + (before[z] + after[z]) + pltpu.roll(here[z], MAXORB, 1)
            out = (band(weight, y, z) - shift) * here[z] - beside
            field[pl.ds(y * BZ + z, 8, stride=BANDS), :] = out
            if with_sum:
                total = total + out * out
        before, here = here, after
    return total


def root_at(k):
    value = jnp.float32(ROOTS[0])
    for i in range(1, len(ROOTS) - 1):
        value = jnp.where(k == i, jnp.float32(ROOTS[i]), value)
    return value


def local_weights(first, second, weight):
    row = iota((16, CELLS), 0)
    stacked = jnp.where(row == 0, first.astype(F32), jnp.where(row == 1, second.astype(F32), jnp.where(row == 2, 1.0, 0.0)))
    stacked = stacked.astype(BF16)
    row, lane = iota((16, LANES), 0), iota((16, LANES), 1)
    spread = jnp.where(row == 2, -3.0, jnp.where((row < 2) & (row == (lane >> 6)), 1.0, 0.0)).astype(BF16)
    for j in range(TILES):
        at = slice(j * LANES, (j + 1) * LANES)
        weight[at, :] = lax.dot_general(
            stacked[:, at], spread, (((0,), (0,)), ((), ())), preferred_element_type=F32
        )


def kernel(
    counts, parity, potential, orbitals, density, filtered,
    loaded, stored, field, weight, next_block, patch, outgoing, incoming,
    load_sem, store_sem, block_sem, send_sem, recv_sem,
):
    g, d = lax.axis_index("grp"), lax.axis_index("dev")
    ahead, behind = lax.rem(d + 1, DEV), lax.rem(d + DEV - 1, DEV)

    def other(k):
        return lax.rem(g + k, GRP)

    loads = [
        pltpu.make_async_copy(orbitals.at[:, :, pl.ds(j * LANES, LANES)], loaded.at[j], load_sem.at[j])
        for j in range(TILES)
    ]
    for copy in loads:
        copy.start()

    barrier = pltpu.get_barrier_semaphore()
    pl.semaphore_signal(barrier, inc=1, device_id=(g, ahead), device_id_type=MESH)

    def greet(k, carry):
        pl.semaphore_signal(barrier, inc=1, device_id=(other(k), behind), device_id_type=MESH)

        @pl.when(k > 0)
        def _():
            pl.semaphore_signal(barrier, inc=1, device_id=(other(k), d), device_id_type=MESH)

        return carry

    lax.fori_loop(0, GRP, greet, 0)

    slots = slot_matrix()
    for copy in loads:
        copy.wait()
    for j in range(TILES):
        tile = loaded[j].reshape(LANES, LANES)
        field[j * LANES : (j + 1) * LANES, :] = lax.dot_general(
            tile, slots, (((0,), (0,)), ((), ())), preferred_element_type=F32
        )

    pl.semaphore_wait(barrier, 2 * GRP)
    block = pltpu.make_async_remote_copy(
        src_ref=potential, dst_ref=next_block, send_sem=block_sem.at[0], recv_sem=block_sem.at[1],
        device_id=(g, behind), device_id_type=MESH,
    )
    block.start()
    block.wait()
    local_weights(potential[...], next_block[...], weight)

    def one(k, carry):
        factor(field, weight, root_at(k), False)
        return carry

    lax.fori_loop(0, len(ROOTS) - 1, one, 0)
    total = factor(field, weight, ROOTS[-1], True)
    total = jnp.sum(total, axis=0, keepdims=True)
    total = total + pltpu.roll(total, MAXORB, 1)
    scale = LEAD * lax.rsqrt(total * (LEAD * LEAD / (2 * CELLS)) + 1e-6)
    live = (iota((1, LANES), 1) & (MAXORB - 1)) < counts[0, d]
    sign = (1 - 2 * parity[0, 0]).astype(F32) / MAXORB

    stores = []
    for j in range(TILES):
        at = slice(j * LANES, (j + 1) * LANES)
        scaled = jnp.where(live, field[at, :] * scale, 0.0).astype(BF16)
        rows = lax.dot_general(slots, scaled, (((1,), (1,)), ((), ())), preferred_element_type=F32)
        stored[j] = rows.astype(BF16).reshape(MAXORB, 2, LANES)
        parts = [rows[8 * i : 8 * i + 8] for i in range(16)]
        parts = [p * p for p in parts]
        while len(parts) > 1:
            parts = [parts[i] + parts[i + 1] for i in range(0, len(parts), 2)]
        dens = parts[0]
        dens = dens + pltpu.roll(dens, 4, 0)
        dens = dens + pltpu.roll(dens, 2, 0)
        patch[:, at] = dens[0:2] * sign
    for j in range(TILES):
        copy = pltpu.make_async_copy(stored.at[j], filtered.at[:, :, pl.ds(j * LANES, LANES)], store_sem.at[j])
        copy.start()
        stores.append(copy)
    for k in range(GRP):
        piece = patch[:, k * SHARE : (k + 1) * SHARE]
        outgoing[0, k] = piece[0:1]
        outgoing[1, k] = piece[1:2]

    def send(kind, k):
        to, there = other(k), (d if kind == 0 else ahead)
        return pltpu.make_async_remote_copy(
            src_ref=outgoing.at[kind, to], dst_ref=incoming.at[kind, g],
            send_sem=send_sem.at[kind, to], recv_sem=recv_sem.at[kind, g],
            device_id=(to, there), device_id_type=MESH,
        )

    def arrival(kind, k):
        source = other(k)
        return pltpu.make_async_remote_copy(
            src_ref=outgoing.at[kind, source], dst_ref=incoming.at[kind, source],
            send_sem=send_sem.at[kind, source], recv_sem=recv_sem.at[kind, source],
            device_id=(source, d), device_id_type=MESH,
        )

    def start(k, carry):
        send(1, k).start()

        @pl.when(k > 0)
        def _():
            send(0, k).start()

        return carry

    lax.fori_loop(0, GRP, start, 0)

    def land(k, carry):
        arrival(1, k).wait_recv()

        @pl.when(k > 0)
        def _():
            arrival(0, k).wait_recv()

        return carry

    lax.fori_loop(0, GRP, land, 0)
    incoming[0, g] = outgoing[0, g]
    density[...] = jnp.sum(incoming[0], axis=0) + jnp.sum(incoming[1], axis=0)

    def leave(k, carry):
        send(1, k).wait_send()

        @pl.when(k > 0)
        def _():
            send(0, k).wait_send()

        return carry

    lax.fori_loop(0, GRP, leave, 0)
    for copy in stores:
        copy.wait()


def on_device(orbitals, potential, counts, parity):
    vmem = pl.BlockSpec(memory_space=pltpu.VMEM)
    smem = pl.BlockSpec(memory_space=pltpu.SMEM)
    hbm = pl.BlockSpec(memory_space=pl.ANY)
    density, filtered = pl.pallas_call(
        kernel,
        in_specs=[smem, smem, vmem, hbm],
        out_specs=[vmem, hbm],
        out_shape=[
            jax.ShapeDtypeStruct((1, SHARE), F32),
            jax.ShapeDtypeStruct((MAXORB, 2, CELLS), BF16),
        ],
        scratch_shapes=[
            pltpu.VMEM((TILES, MAXORB, 2, LANES), BF16),
            pltpu.VMEM((TILES, MAXORB, 2, LANES), BF16),
            pltpu.VMEM((CELLS, LANES), F32),
            pltpu.VMEM((CELLS, LANES), F32),
            pltpu.VMEM((1, CELLS), BF16),
            pltpu.VMEM((2, CELLS), F32),
            pltpu.VMEM((2, GRP, 1, SHARE), F32),
            pltpu.VMEM((2, GRP, 1, SHARE), F32),
            pltpu.SemaphoreType.DMA((TILES,)),
            pltpu.SemaphoreType.DMA((TILES,)),
            pltpu.SemaphoreType.DMA((2,)),
            pltpu.SemaphoreType.DMA((2, GRP)),
            pltpu.SemaphoreType.DMA((2, GRP)),
        ],
        compiler_params=pltpu.CompilerParams(collective_id=0, has_side_effects=True),
        name="filter_and_assemble",
    )(counts, parity, potential, orbitals[0, 0])
    return density[None], filtered[None, None]


def solution(mesh):
    placed = (P("grp", "dev", None, None, None), P("dev", None), P("grp", None), P("grp", "dev"))
    return jax.shard_map(
        on_device,
        mesh=mesh,
        in_specs=placed,
        out_specs=(P("dev", None, "grp"), P("grp", "dev", None, None, None)),
        check_vma=False,
    )
```

profile of v0, /device:TPU:1, one launch (start us, length us, event | category | flops | bytes accessed | tf_op | source)
XLA Modules:
  0.0 43.3 jit_solution(15627222633524770583)
XLA Ops:
  1.3 38.5 %filter_and_assemble.1 = (f32[1,144]{1,0:T(1,128)}, bf16[64,2,2304]{2,1,0:T(2,128)(2,1)}) custom-call(s32[1,64]{1,0:T(1,128)} %counts.1, s32[1,1]{1,0:T(1,128)S(6)} %copy.8.parity, bf16[1,2304]{1,0:T(2,128)(2,1)} %potential.1, bf16[64,2,2304]{2,1,0:T(2,128)(2,1)} %bitcast.3), custom_call_target="tpu_custom_call" | custom-call | tf_op jit(solution)/shard_map/filter_and_assemble/pallas_call | solution.py:226
  39.8 0.0 copy-start
  39.8 0.7 %copy-done = f32[1,144]{1,0:T(1,128)S(1)} copy-done((f32[1,144]{1,0:T(1,128)S(1)}, f32[1,144]{1,0:T(1,128)}, u32[]{:S(2)}) %copy-start) | copy-done | bytes 600
  40.4 0.6 %copy.9 = f32[1,1,144]{2,1,0:T(1,128)} copy(f32[1,1,144]{2,1,0:T(1,128)S(1)} %bitcast.5) | data formatting | bytes 1152
  41.0 2.3 %copy.10 = bf16[1,1,64,2,2304]{4,3,2,1,0:T(2,128)(2,1)} copy(bf16[1,1,64,2,2304]{4,3,2,1,0:T(2,128)(2,1)} %bitcast.4) | data formatting | bytes 1179648
Async XLA Ops:
  39.8 0.7 %copy-start = (f32[1,144]{1,0:T(1,128)S(1)}, f32[1,144]{1,0:T(1,128)}, u32[]{:S(2)}) copy-start(f32[1,144]{1,0:T(1,128)} %get-tuple-element.4) | copy-start | bytes 1732
where the time goes:
time: 43.6 us; the launch traced here: 43.3 us
  Pallas kernels  38.5 us (88%)
  local copies, waits for them, and re-layouts  3.5 us (8%)
  between operations  1.29 us (3%)
    pallas_call x1, Pallas kernels, on_device(): pl.pallas_call(kernel, in_specs=[smem, smem, vmem, hbm], out_specs=[vmem,...  38.5 us
    unnamed x4, local copies, waits for them, and re-layouts  3.5 us

commit v1 on v0

v1 whole, which is shorter than its diff:
```python
import functools
import math

import jax
import jax.numpy as jnp
from jax import lax
from jax.experimental import pallas as pl
from jax.experimental.pallas import tpu as pltpu
from jax.sharding import PartitionSpec as P

MAXORB = 64
CELLS = 2304
BZ = 48
ROWS = 48
BANDS = 6
TILES = 18
LANES = 128
SHARE = 144
GRP = 16
DEV = 64
ROOTS = [math.cos((2 * i - 1) * math.pi / 16) for i in (1, 8, 4, 5, 2, 7, 3, 6)]
LEAD = 2.0**7 / 7.0**8
MESH = pl.DeviceIdType.MESH
F32 = jnp.float32
BF16 = jnp.bfloat16


def iota(shape, dim):
    return lax.broadcasted_iota(jnp.int32, shape, dim)


def slot_matrix():
    row, lane = iota((LANES, LANES), 0), iota((LANES, LANES), 1)
    return jnp.where((row >> 1) + (row & 1) * MAXORB == lane, 1.0, 0.0).astype(BF16)


def band(ref, y, zi):
    return ref[pl.ds(y * BZ + zi, 8, stride=BANDS), :]


def factor(field, weight, root, with_sum):
    sub = iota((8, LANES), 0)
    first, last = sub == 0, sub == 7
    shift = 7.0 * root
    zero = jnp.zeros((8, LANES), F32)
    before, here = [zero] * BANDS, [band(field, 0, z) for z in range(BANDS)]
    total = zero
    for y in range(ROWS):
        after = [band(field, y + 1, z) for z in range(BANDS)] if y + 1 < ROWS else [zero] * BANDS
        low = jnp.where(first, 0.0, pltpu.roll(here[-1], 1, 0))
        high = jnp.where(last, 0.0, pltpu.roll(here[0], 7, 0))
        wide = [low] + here + [high]
        for z in range(BANDS):
            beside = (wide[z] + wide[z + 2]) + (before[z] + after[z]) + pltpu.roll(here[z], MAXORB, 1)
            out = (band(weight, y, z) - shift) * here[z] - beside
            field[pl.ds(y * BZ + z, 8, stride=BANDS), :] = out
            if with_sum:
                total = total + out * out
        before, here = here, after
    return total


def local_weights(first, second, weight):
    row = iota((16, CELLS), 0)
    stacked = jnp.where(row == 0, first.astype(F32), jnp.where(row == 1, second.astype(F32), jnp.where(row == 2, 1.0, 0.0)))
    stacked = stacked.astype(BF16)
    row, lane = iota((16, LANES), 0), iota((16, LANES), 1)
    spread = jnp.where(row == 2, -3.0, jnp.where((row < 2) & (row == (lane >> 6)), 1.0, 0.0)).astype(BF16)
    for j in range(TILES):
        at = slice(j * LANES, (j + 1) * LANES)
        weight[at, :] = lax.dot_general(
            stacked[:, at], spread, (((0,), (0,)), ((), ())), preferred_element_type=F32
        )


def kernel(
    counts, parity, potential, orbitals, density, stored,
    loaded, field, weight, own, next_block, patch, outgoing, incoming, count_row, parity_bit,
    load_sem, small_sem, block_sem, send_sem, recv_sem,
):
    g, d = lax.axis_index("grp"), lax.axis_index("dev")
    ahead, behind = lax.rem(d + 1, DEV), lax.rem(d + DEV - 1, DEV)

    def other(k):
        return lax.rem(g + k, GRP)

    barrier = pltpu.get_barrier_semaphore()
    pl.semaphore_signal(barrier, inc=1, device_id=(g, ahead), device_id_type=MESH)

    def greet(k, carry):
        pl.semaphore_signal(barrier, inc=1, device_id=(other(k), behind), device_id_type=MESH)

        @pl.when(k > 0)
        def _():
            pl.semaphore_signal(barrier, inc=1, device_id=(other(k), d), device_id_type=MESH)

        return carry

    lax.fori_loop(0, GRP, greet, 0)

    small = [
        pltpu.make_async_copy(potential, own, small_sem.at[0]),
        pltpu.make_async_copy(counts, count_row, small_sem.at[1]),
        pltpu.make_async_copy(parity, parity_bit, small_sem.at[2]),
    ]
    for copy in small:
        copy.start()
    loads = [
        pltpu.make_async_copy(orbitals.at[:, :, pl.ds(j * LANES, LANES)], loaded.at[j], load_sem.at[j])
        for j in range(TILES)
    ]
    for copy in loads:
        copy.start()

    small[0].wait()
    pl.semaphore_wait(barrier, 2 * GRP)
    block = pltpu.make_async_remote_copy(
        src_ref=own, dst_ref=next_block, send_sem=block_sem.at[0], recv_sem=block_sem.at[1],
        device_id=(g, behind), device_id_type=MESH,
    )
    block.start()

    slots = slot_matrix()
    for copy in loads:
        copy.wait()
    for j in range(TILES):
        tile = loaded[j].reshape(LANES, LANES)
        field[j * LANES : (j + 1) * LANES, :] = lax.dot_general(
            tile, slots, (((0,), (0,)), ((), ())), preferred_element_type=F32
        )

    block.wait_recv()
    local_weights(own[...], next_block[...], weight)

    for root in ROOTS[:-1]:
        factor(field, weight, root, False)
    total = factor(field, weight, ROOTS[-1], True)
    total = jnp.sum(total, axis=0, keepdims=True)
    total = total + pltpu.roll(total, MAXORB, 1)
    scale = LEAD * lax.rsqrt(total * (LEAD * LEAD / (2 * CELLS)) + 1e-6)
    small[1].wait()
    small[2].wait()
    live = (iota((1, LANES), 1) & (MAXORB - 1)) < count_row[0, d]
    sign = (1 - 2 * parity_bit[0, 0]).astype(F32) / MAXORB

    def send(kind, k):
        there = d if kind == 0 else ahead
        return pltpu.make_async_remote_copy(
            src_ref=outgoing.at[kind, k], dst_ref=incoming.at[kind, g],
            send_sem=send_sem.at[kind, k], recv_sem=recv_sem.at[kind, g],
            device_id=(k, there), device_id_type=MESH,
        )

    def arrival(kind, source):
        return pltpu.make_async_remote_copy(
            src_ref=outgoing.at[kind, source], dst_ref=incoming.at[kind, source],
            send_sem=send_sem.at[kind, source], recv_sem=recv_sem.at[kind, source],
            device_id=(source, d), device_id_type=MESH,
        )

    def begin(k, carry):
        send(1, k).start()

        @pl.when(k != g)
        def _():
            send(0, k).start()

        return carry

    for tiles, pieces in ((range(0, 5), range(0, 4)), (range(5, TILES), range(4, GRP))):
        for j in tiles:
            at = slice(j * LANES, (j + 1) * LANES)
            scaled = jnp.where(live, field[at, :] * scale, 0.0).astype(BF16)
            rows = lax.dot_general(slots, scaled, (((1,), (1,)), ((), ())), preferred_element_type=F32)
            stored[j] = rows.astype(BF16).reshape(MAXORB, 2, LANES)
            parts = [rows[8 * i : 8 * i + 8] for i in range(16)]
            parts = [p * p for p in parts]
            while len(parts) > 1:
                parts = [parts[i] + parts[i + 1] for i in range(0, len(parts), 2)]
            dens = parts[0]
            dens = dens + pltpu.roll(dens, 4, 0)
            dens = dens + pltpu.roll(dens, 2, 0)
            patch[:, at] = dens[0:2] * sign
        for k in pieces:
            piece = patch[:, k * SHARE : (k + 1) * SHARE]
            outgoing[0, k] = piece[0:1]
            outgoing[1, k] = piece[1:2]
        lax.fori_loop(pieces[0], pieces[-1] + 1, begin, 0)

    def land(k, carry):
        arrival(1, k).wait_recv()

        @pl.when(k != g)
        def _():
            arrival(0, k).wait_recv()

        return carry

    lax.fori_loop(0, GRP, land, 0)
    incoming[0, g] = outgoing[0, g]
    density[...] = jnp.sum(incoming[0], axis=0) + jnp.sum(incoming[1], axis=0)

    def leave(k, carry):
        send(1, k).wait_send()

        @pl.when(k != g)
        def _():
            send(0, k).wait_send()

        return carry

    lax.fori_loop(0, GRP, leave, 0)
    block.wait_send()

def deliver(share, stored, density, filtered, sem):
    copies = [
        pltpu.make_async_copy(stored.at[j], filtered.at[:, :, pl.ds(j * LANES, LANES)], sem.at[j])
        for j in range(TILES)
    ]
    copies.append(pltpu.make_async_copy(share, density, sem.at[TILES]))
    for copy in copies:
        copy.start()
    for copy in copies:
        copy.wait()


def on_device(orbitals, potential, counts, parity):
    vmem = pl.BlockSpec(memory_space=pltpu.VMEM)
    hbm = pl.BlockSpec(memory_space=pl.ANY)
    share, stored = pl.pallas_call(
        kernel,
        in_specs=[pl.BlockSpec(memory_space=pltpu.HBM)] * 4,
        out_specs=[vmem, vmem],
        out_shape=[
            pltpu.VMEM((1, SHARE), F32),
            pltpu.VMEM((TILES, MAXORB, 2, LANES), BF16),
        ],
        scratch_shapes=[
            pltpu.VMEM((TILES, MAXORB, 2, LANES), BF16),
            pltpu.VMEM((CELLS, LANES), F32),
            pltpu.VMEM((CELLS, LANES), F32),
            pltpu.VMEM((1, CELLS), BF16),
            pltpu.VMEM((1, CELLS), BF16),
            pltpu.VMEM((2, CELLS), F32),
            pltpu.VMEM((2, GRP, 1, SHARE), F32),
            pltpu.VMEM((2, GRP, 1, SHARE), F32),
            pltpu.SMEM((1, DEV), jnp.int32),
            pltpu.SMEM((1, 1), jnp.int32),
            pltpu.SemaphoreType.DMA((TILES,)),
            pltpu.SemaphoreType.DMA((3,)),
            pltpu.SemaphoreType.DMA((2,)),
            pltpu.SemaphoreType.DMA((2, GRP)),
            pltpu.SemaphoreType.DMA((2, GRP)),
        ],
        compiler_params=pltpu.CompilerParams(collective_id=0, has_side_effects=True),
        name="filter_and_assemble",
    )(counts, parity, potential, orbitals[0, 0])
    density, filtered = pl.pallas_call(
        deliver,
        in_specs=[vmem, vmem],
        out_specs=[hbm, hbm],
        out_shape=[
            jax.ShapeDtypeStruct((1, SHARE), F32),
            jax.ShapeDtypeStruct((MAXORB, 2, CELLS), BF16),
        ],
        scratch_shapes=[pltpu.SemaphoreType.DMA((TILES + 1,))],
        name="deliver",
    )(pltpu.with_memory_space_constraint(share, pltpu.VMEM), pltpu.with_memory_space_constraint(stored, pltpu.VMEM))
    return density[None], filtered[None, None]


def solution(mesh):
    placed = (P("grp", "dev", None, None, None), P("dev", None), P("grp", None), P("grp", "dev"))
    return jax.shard_map(
        on_device,
        mesh=mesh,
        in_specs=placed,
        out_specs=(P("dev", None, "grp"), P("grp", "dev", None, None, None)),
        check_vma=False,
    )
```

time: 43.6 us -> 38.7 us (0.89)
  local copies, waits for them, and re-layouts: 3.5 us -> 0 us
  Pallas kernels: 38.5 us -> 37.2 us
    unnamed x4 -> x0, local copies, waits for them, and re-layouts: 3.5 us -> none
    pallas_call x1 -> x2, Pallas kernels: 38.5 us -> 37.2 us  [the longest x1 36.2 us: on_device(): pl.pallas_call(kernel, in_specs=[pl.BlockSpec(memory_space=pltpu.HBM)] *...]
where the time goes in v1:
time: 38.7 us; the launch traced here: 38.4 us
  Pallas kernels  37.2 us (96%)
  between operations  1.29 us (3%)
    pallas_call x1, Pallas kernels, on_device(): pl.pallas_call(kernel, in_specs=[pl.BlockSpec(memory_space=pltpu.HBM)] *...  36.2 us
    pallas_call x1, Pallas kernels, on_device(): pl.pallas_call(deliver, in_specs=[vmem, vmem], out_specs=[hbm, hbm], out_...  0.97 us

profile of v1, /device:TPU:1, one launch (start us, length us, event | category | flops | bytes accessed | tf_op | source)
XLA Modules:
  0.0 38.4 jit_solution(15114003672703755036)
XLA Ops:
  1.3 36.2 %filter_and_assemble.1 = (f32[1,144]{1,0:T(1,128)S(1)}, bf16[18,64,2,128]{3,2,1,0:T(2,128)(2,1)S(1)}) custom-call(s32[1,64]{1,0:T(1,128)} %counts.1, s32[1,1]{1,0:T(1,128)S(6)} %copy.6.parity, bf16[1,2304]{1,0:T(2,128)(2,1)} %potential.1, bf16[64,2,2304]{2,1,0:T(2,128)(2,1)} %bitcast.3), custom_call_target="tpu_custom_call" | custom-call | tf_op jit(solution)/shard_map/filter_and_assemble/pallas_call | solution.py:230
  37.5 1.0 %deliver.1 = (f32[1,144]{1,0:T(1,128)}, bf16[64,2,2304]{2,1,0:T(2,128)(2,1)}) custom-call(f32[1,144]{1,0:T(1,128)S(1)} %get-tuple-element.6.share, bf16[18,64,2,128]{3,2,1,0:T(2,128)(2,1)S(1)} %get-tuple-element.7.stored), custom_call_target="tpu_custom_call" | custom-call | tf_op jit(solution)/shard_map/deliver/pallas_call | solution.py:258
